TPU v7x, 32 devices: a whole 2x2x4 slice. The times are simulated.
32 devices in a mesh: wide: 8 (over z, x), narrow: 4 (over y, core).
Axes of the slice: x: 2, y: 2, z: 4, core: 2. Of those that a mesh axis runs over, the one named last changes fastest.
Arguments:
- points: bfloat16 [32768, 256], P('wide'), may hold values from -6 to 6
- q_init: float32 [16, 32768], P(None, 'wide'), may hold values from -80 to 80
- pairs: int32 [2, 2048], P(None, ('wide', 'narrow')), may hold values from 0 to 255, as said below
Outputs:
- basis: float32 [16, 32768], P(None, 'wide')
- coeffs: float32 [3, 2, 16, 16], replicated
Inputs may be any that keep to these rules, and one draw needn't show every extreme that they name: `pairs`: pair number g * 4 * 64 + m * 64 + o * 8 + c (g < 8, m < 4, o < 8, c < 8) has its first block in g * 32 .. (g + 1) * 32 - 1 and its second block in o * 32 .. (o + 1) * 32 - 1; the two ends of a pair differ.
All inputs are finite; a program needn't handle non-finite values.
Results may differ from a plain program's by a relative error of at most 0.0015.
Values may be sent and summed in bfloat16 or wider, within the bound.
A program may use at most 64 MiB of HBM per device.

v0:
```python
import jax
import jax.numpy as jnp
from jax import lax
from jax.sharding import PartitionSpec as P

BS = 128
STEPS = 3
KERNEL_FACTOR = 3.0
EPSILON = 1e-06
HIGH = lax.Precision.HIGHEST
pair_group = 32


def unit_rows(points):
    wide32 = points.astype(jnp.float32)
    scaled = wide32 * lax.rsqrt(jnp.sum(wide32 * wide32, axis=-1, keepdims=True) + EPSILON)
    return scaled.astype(jnp.bfloat16)


def tile_terms(first_pts, second_pts, first_vec, second_vec):
    inner_products = jnp.einsum(
        "paf,pbf->pab", first_pts, second_pts, preferred_element_type=jnp.float32
    )
    kernel_values = jnp.exp(KERNEL_FACTOR * (inner_products - 1.0))
    to_first = jnp.einsum("pab,prb->pra", kernel_values, second_vec, precision=HIGH)
    to_second = jnp.einsum("pab,pra->prb", kernel_values, first_vec, precision=HIGH)
    return (to_first, to_second)


def per_device(points, q_init, pairs):
    wide_count = lax.axis_size("wide")
    wide_pos = lax.axis_index("wide")
    own_blocks = points.shape[0] // BS
    width = points.shape[1]
    vec_rows = q_init.shape[0]
    pair_count = pairs.shape[1]
    capacity = pair_count // wide_count
    total_points = own_blocks * BS * wide_count
    unit = unit_rows(points).reshape(own_blocks, BS, width)
    first_local = pairs[0] - wide_pos * own_blocks
    wanted = pairs[1].reshape(wide_count, capacity)
    local_ids = (
        lax.all_to_all(wanted, "wide", split_axis=0, concat_axis=0, tiled=True)
        - wide_pos * own_blocks
    )
    replies = lax.all_to_all(unit[local_ids], "wide", split_axis=0, concat_axis=0, tiled=True)
    second_pts = replies
    second_pts = second_pts.reshape(pair_count, BS, width)
    targets = jnp.concatenate([first_local, local_ids.reshape(pair_count)], axis=0)
    owners = (jnp.arange(own_blocks, dtype=jnp.int32)[:, None] == targets[None, :]).astype(
        jnp.float32
    )

    def grouped(values):
        return values.reshape((pair_count // pair_group, pair_group) + values.shape[1:])

    def single_group(items):
        first_ids, second_p, first_v, second_v = items
        return tile_terms(unit[first_ids], second_p, first_v, second_v)

    def gram_sums(values):
        return lax.psum(values, "wide")

    gram0 = gram_sums(jnp.dot(q_init, q_init.T, precision=HIGH)) / total_points
    factor0 = jnp.linalg.cholesky(gram0)
    present_portion = lax.linalg.triangular_solve(factor0, q_init, left_side=True, lower=True)
    current = present_portion
    previous = jnp.zeros_like(present_portion)
    last = jnp.zeros((vec_rows, vec_rows), jnp.float32)
    records = []
    for step in range(STEPS):
        rows = current.reshape(vec_rows, own_blocks, BS).transpose(1, 0, 2)
        second_vec = lax.all_to_all(
            rows[local_ids], "wide", split_axis=0, concat_axis=0, tiled=True
        ).reshape(pair_count, vec_rows, BS)
        first_vec = rows[first_local]
        to_first, to_second = lax.map(
            single_group,
            (grouped(first_local), grouped(second_pts), grouped(first_vec), grouped(second_vec)),
        )
        to_first = to_first.reshape(pair_count, vec_rows * BS)
        returned = lax.all_to_all(
            to_second.reshape(wide_count, capacity, vec_rows * BS),
            "wide",
            split_axis=0,
            concat_axis=0,
            tiled=True,
        )
        terms = jnp.concatenate([to_first, returned.reshape(pair_count, vec_rows * BS)], axis=0)
        summed_blocks = jnp.dot(owners, terms, precision=HIGH)
        summed_blocks = lax.psum(summed_blocks, "narrow")
        image = summed_blocks.reshape(-1, vec_rows, BS).transpose(1, 0, 2).reshape(vec_rows, -1)
        residual = image - jnp.dot(last.T, previous, precision=HIGH)
        raw, cross, basis_gram = gram_sums(
            (
                jnp.dot(residual, residual.T, precision=HIGH),
                jnp.dot(present_portion, residual.T, precision=HIGH),
                jnp.dot(present_portion, present_portion.T, precision=HIGH),
            )
        )
        along = cross / total_points
        raw = raw / total_points
        basis_gram = basis_gram / total_points
        remainder = residual - jnp.dot(along.T, present_portion, precision=HIGH)
        squared = jnp.dot(along.T, along, precision=HIGH)
        gram = (
            raw
            - 2.0 * squared
            + jnp.dot(along.T, jnp.dot(basis_gram, along, precision=HIGH), precision=HIGH)
        )
        factor = jnp.linalg.cholesky(gram)
        records.append(jnp.stack([along, factor]))
        previous = present_portion
        last = factor
        present_portion = lax.linalg.triangular_solve(factor, remainder, left_side=True, lower=True)
        current = present_portion
    return (current, jnp.stack(records))


def solution(mesh):
    placed = (P("wide", None), P(None, "wide"), P(None, ("wide", "narrow")))
    return jax.shard_map(
        per_device, mesh=mesh, in_specs=placed, out_specs=(P(None, "wide"), P()), check_vma=False
    )
```

profile of v0, /device:TPU:0, one launch (start us, length us, event | category | flops | bytes accessed | tf_op | source)
XLA Modules:
  0.0 559.8 jit_solution(13503507722654973966)
XLA Ops:
  8.6 7.3 %all-to-all-start = ((s32[8,1,8]{2,1,0:T(1,128)}), s32[8,1,8]{2,1,0:T(1,128)S(1)}, u32[]{:S(2)}, u32[]{:S(2)}) async-start(s32[8,1,8]{2,1,0:T(1,128)} %bitcast.22), calls=%async_computation | async-start | bytes 8192 | tf_op jit(solution)/shard_map/all_to_all | solution.py:43
  16.4 22.1 %psum.91 = f32[16,16]{1,0:T(8,128)S(1)} all-reduce(f32[16,16]{1,0:T(8,128)S(1)} %fusion.187), channel_id=1, replica_groups=mesh['wide'=8,'narrow'=4] {'wide'}, use_global_device_ids=true, to_apply=%region_1.0 | all-reduce | flops 256 | bytes 2048 | tf_op jit(solution)/shard_map/psum | solution.py:62
  55.1 5.6 %all-to-all-done.1 = f32[8,8,16,128]{3,2,1,0:T(8,128)S(1)} async-done(((f32[8,8,16,128]{3,2,1,0:T(8,128)}), f32[8,8,16,128]{3,2,1,0:T(8,128)S(1)}, u32[]{:S(2)}, u32[]{:S(2)}) %all-to-all-start.1) | async-done | bytes 524320 | tf_op jit(solution)/shard_map/all_to_all | solution.py:73
  60.7 4.7 all-to-all-start.2
  67.0 87.2 %all-to-all-done.2 = bf16[8,8,128,256]{3,2,1,0:T(8,128)(2,1)} async-done(((bf16[8,8,128,256]{3,2,1,0:T(8,128)(2,1)}), bf16[8,8,128,256]{3,2,1,0:T(8,128)(2,1)}, u32[]{:S(2)}, u32[]{:S(2)}) %all-to-all-start.2) | async-done | bytes 4194336 | tf_op jit(solution)/shard_map/all_to_all | solution.py:46
  155.9 23.6 %while.42 = (s32[]{:T(128)}, f32[2,32,16,128]{3,2,1,0:T(8,128)}, f32[2,32,16,128]{3,2,1,0:T(8,128)}, f32[2,32,16,128]{3,2,1,0:T(8,128)S(1)}, s32[2,32]{1,0:T(2,1...) while((s32[]{:T(128)}, f32[2,32,16,128]{3,2,1,0:T(8,128)}, ...), condition=%wide.region_5.8_spmd, body=%wide.region_4.7_spmd.sunk | while | flops 471860320 | bytes 17833084 | solution.py:77
  187.2 12.4 %all-to-all-done.3 = f32[8,8,2048]{2,1,0:T(8,128)S(1)} async-done(((f32[8,8,2048]{2,1,0:T(8,128)}), f32[8,8,2048]{2,1,0:T(8,128)S(1)}, u32[]{:S(2)}, u32[]{:S(2)}) %all-to-all-start.3) | async-done | bytes 524320 | tf_op jit(solution)/shard_map/all_to_all | solution.py:82
  202.4 31.1 %all-reduce.7.cloned.1.call-done = f32[16,4096]{1,0:T(8,128)} async-done(((f32[16,4096]{1,0:T(8,128)}), f32[16,4096]{1,0:T(8,128)}) %all-reduce.7.cloned.1.call-update) | async-done | bytes 262160 | tf_op jit(solution)/shard_map/psum | solution.py:91
  235.6 37.1 %all-reduce.2 = (f32[16,16]{1,0:T(8,128)S(1)}, f32[16,16]{1,0:T(8,128)S(1)}, f32[16,16]{1,0:T(8,128)S(1)}) all-reduce(f32[16,16]{1,0:T(8,128)S(1)} %fusion.189, f32[16,16]{1,0:T(8,128)S(1)} %fusion.188, f32[16,16]{1,0:T(8,128)S(1)} %fusion.190), channel_id=1, replica_groups=mesh['wide'=8,'narrow'=4] {'wide'}, use_global_device_ids=true, to_apply=%region_8.11 | all-reduce | flops 768 | bytes 6144 | tf_op jit(solution)/shard_map/psum | solution.py:62
  285.3 8.8 %all-to-all-done.4 = f32[8,8,16,128]{3,2,1,0:T(8,128)} async-done(((f32[8,8,16,128]{3,2,1,0:T(8,128)}), f32[8,8,16,128]{3,2,1,0:T(8,128)}, u32[]{:S(2)}, u32[]{:S(2)}) %all-to-all-start.4) | async-done | bytes 524320 | tf_op jit(solution)/shard_map/all_to_all | solution.py:73
  295.8 25.6 %while.43 = (s32[]{:T(128)}, f32[2,32,16,128]{3,2,1,0:T(8,128)}, f32[2,32,16,128]{3,2,1,0:T(8,128)}, f32[2,32,16,128]{3,2,1,0:T(8,128)}, s32[2,32]{1,0:T(2,128)S...) while((s32[]{:T(128)}, f32[2,32,16,128]{3,2,1,0:T(8,128)}, ...), condition=%wide.region_11.14_spmd, body=%wide.region_10.13_spmd.sunk | while | flops 471860320 | bytes 17833084 | solution.py:77
  300.7 5.1 fusion.273
  313.5 5.1 fusion.273
  329.0 8.2 %all-to-all-done.5 = f32[8,8,2048]{2,1,0:T(8,128)S(1)} async-done(((f32[8,8,2048]{2,1,0:T(8,128)}), f32[8,8,2048]{2,1,0:T(8,128)S(1)}, u32[]{:S(2)}, u32[]{:S(2)}) %all-to-all-start.5) | async-done | bytes 524320 | tf_op jit(solution)/shard_map/all_to_all | solution.py:82
  339.9 30.2 %all-reduce.9.cloned.1.call-done = f32[16,4096]{1,0:T(8,128)} async-done(((f32[16,4096]{1,0:T(8,128)}), f32[16,4096]{1,0:T(8,128)}) %all-reduce.9.cloned.1.call-update) | async-done | bytes 262160 | tf_op jit(solution)/shard_map/psum | solution.py:91
  373.0 37.1 %all-reduce.1 = (f32[16,16]{1,0:T(8,128)S(1)}, f32[16,16]{1,0:T(8,128)S(1)}, f32[16,16]{1,0:T(8,128)S(1)}) all-reduce(f32[16,16]{1,0:T(8,128)S(1)} %fusion.192, f32[16,16]{1,0:T(8,128)S(1)} %fusion.191, f32[16,16]{1,0:T(8,128)S(1)} %fusion.193), channel_id=1, replica_groups=mesh['wide'=8,'narrow'=4] {'wide'}, use_global_device_ids=true, to_apply=%region_14.17 | all-reduce | flops 768 | bytes 6144 | tf_op jit(solution)/shard_map/psum | solution.py:62
  417.0 4.4 all-to-all-start.6
  422.8 8.6 %all-to-all-done.6 = f32[8,8,16,128]{3,2,1,0:T(8,128)} async-done(((f32[8,8,16,128]{3,2,1,0:T(8,128)}), f32[8,8,16,128]{3,2,1,0:T(8,128)}, u32[]{:S(2)}, u32[]{:S(2)}) %all-to-all-start.6) | async-done | bytes 524320 | tf_op jit(solution)/shard_map/all_to_all | solution.py:73
  433.1 25.6 %while.44 = (s32[]{:T(128)}, f32[2,32,16,128]{3,2,1,0:T(8,128)}, f32[2,32,16,128]{3,2,1,0:T(8,128)}, f32[2,32,16,128]{3,2,1,0:T(8,128)}, s32[2,32]{1,0:T(2,128)S...) while((s32[]{:T(128)}, f32[2,32,16,128]{3,2,1,0:T(8,128)}, ...), condition=%wide.region_17.20_spmd, body=%wide.region_16.19_spmd.sunk | while | flops 471860320 | bytes 17833084 | solution.py:77
  438.0 5.1 fusion.281
  450.8 5.1 fusion.281
  466.0 8.5 %all-to-all-done.7 = f32[8,8,2048]{2,1,0:T(8,128)S(1)} async-done(((f32[8,8,2048]{2,1,0:T(8,128)}), f32[8,8,2048]{2,1,0:T(8,128)S(1)}, u32[]{:S(2)}, u32[]{:S(2)}) %all-to-all-start.7) | async-done | bytes 524320 | tf_op jit(solution)/shard_map/all_to_all | solution.py:82
  475.8 30.6 %all-reduce.11.cloned.1.call-done = f32[16,4096]{1,0:T(8,128)} async-done(((f32[16,4096]{1,0:T(8,128)}), f32[16,4096]{1,0:T(8,128)}) %all-reduce.11.cloned.1.call-update) | async-done | bytes 262160 | tf_op jit(solution)/shard_map/psum | solution.py:91
  509.3 37.1 %all-reduce = (f32[16,16]{1,0:T(8,128)S(1)}, f32[16,16]{1,0:T(8,128)S(1)}, f32[16,16]{1,0:T(8,128)S(1)}) all-reduce(f32[16,16]{1,0:T(8,128)S(1)} %fusion.195, f32[16,16]{1,0:T(8,128)S(1)} %fusion.194, f32[16,16]{1,0:T(8,128)S(1)} %fusion.196), channel_id=1, replica_groups=mesh['wide'=8,'narrow'=4] {'wide'}, use_global_device_ids=true, to_apply=%region_20.23 | all-reduce | flops 768 | bytes 6144 | tf_op jit(solution)/shard_map/psum | solution.py:62
  (171 shorter events, 144.3 us)
Async XLA Ops:
  7.2 8.8 %copy-start = (f32[16,4096]{1,0:T(8,128)S(1)}, f32[16,4096]{1,0:T(8,128)}, u32[]{:S(2)}) copy-start(f32[16,4096]{1,0:T(8,128)} %param.13) | copy-start | bytes 786436
  8.6 36.7 %all-to-all-start = ((s32[8,1,8]{2,1,0:T(1,128)}), s32[8,1,8]{2,1,0:T(1,128)S(1)}, u32[]{:S(2)}, u32[]{:S(2)}) async-start(s32[8,1,8]{2,1,0:T(1,128)} %bitcast.22), calls=%async_computation | async-start | bytes 8192 | tf_op jit(solution)/shard_map/all_to_all | solution.py:43
  46.9 13.9 %all-to-all-start.1 = ((f32[8,8,16,128]{3,2,1,0:T(8,128)}), f32[8,8,16,128]{3,2,1,0:T(8,128)S(1)}, u32[]{:S(2)}, u32[]{:S(2)}) async-start(f32[8,8,16,128]{3,2,1,0:T(8,128)} %bitcast.29), calls=%async_computation.1 | async-start | bytes 1048576 | tf_op jit(solution)/shard_map/all_to_all | solution.py:73
  60.7 4.7 copy-start.4
  60.7 93.5 %all-to-all-start.2 = ((bf16[8,8,128,256]{3,2,1,0:T(8,128)(2,1)}), bf16[8,8,128,256]{3,2,1,0:T(8,128)(2,1)}, u32[]{:S(2)}, u32[]{:S(2)}) async-start(bf16[8,8,128,256]{3,2,1,0:T(8,128)(2,1)} %bitcast.312), calls=%async_computation.2 | async-start | bytes 8388608 | tf_op jit(solution)/shard_map/all_to_all | solution.py:46
  160.9 4.1 copy-start.2
  172.7 4.1 copy-start.2
  181.5 18.2 %all-to-all-start.3 = ((f32[8,8,2048]{2,1,0:T(8,128)}), f32[8,8,2048]{2,1,0:T(8,128)S(1)}, u32[]{:S(2)}, u32[]{:S(2)}) async-start(f32[8,8,2048]{2,1,0:T(8,128)} %reshape.254), calls=%async_computation.3 | async-start | bytes 1048576 | tf_op jit(solution)/shard_map/all_to_all | solution.py:82
  185.0 48.6 %all-reduce.7.cloned.1.call-start = ((), (), s32[]{:S(2)}) async-start(), calls=%async_computation.8 | async-start | bytes 524288 | tf_op jit(solution)/shard_map/psum | solution.py:91
  279.7 14.4 %all-to-all-start.4 = ((f32[8,8,16,128]{3,2,1,0:T(8,128)}), f32[8,8,16,128]{3,2,1,0:T(8,128)}, u32[]{:S(2)}, u32[]{:S(2)}) async-start(f32[8,8,16,128]{3,2,1,0:T(8,128)} %bitcast.324), calls=%async_computation.4 | async-start | bytes 1048576 | tf_op jit(solution)/shard_map/all_to_all | solution.py:73
  300.7 5.1 copy-start.3
  313.5 5.1 copy-start.3
  323.2 13.9 %all-to-all-start.5 = ((f32[8,8,2048]{2,1,0:T(8,128)}), f32[8,8,2048]{2,1,0:T(8,128)S(1)}, u32[]{:S(2)}, u32[]{:S(2)}) async-start(f32[8,8,2048]{2,1,0:T(8,128)} %reshape.261), calls=%async_computation.5 | async-start | bytes 1048576 | tf_op jit(solution)/shard_map/all_to_all | solution.py:82
  326.9 43.2 %all-reduce.9.cloned.1.call-start = ((), (), s32[]{:S(2)}) async-start(), calls=%async_computation.9 | async-start | bytes 524288 | tf_op jit(solution)/shard_map/psum | solution.py:91
  417.0 14.4 %all-to-all-start.6 = ((f32[8,8,16,128]{3,2,1,0:T(8,128)}), f32[8,8,16,128]{3,2,1,0:T(8,128)}, u32[]{:S(2)}, u32[]{:S(2)}) async-start(f32[8,8,16,128]{3,2,1,0:T(8,128)} %bitcast.323), calls=%async_computation.6 | async-start | bytes 1048576 | tf_op jit(solution)/shard_map/all_to_all | solution.py:73
  438.0 5.1 copy-start.1
  450.8 5.1 copy-start.1
  460.6 13.9 %all-to-all-start.7 = ((f32[8,8,2048]{2,1,0:T(8,128)}), f32[8,8,2048]{2,1,0:T(8,128)S(1)}, u32[]{:S(2)}, u32[]{:S(2)}) async-start(f32[8,8,2048]{2,1,0:T(8,128)} %reshape.268), calls=%async_computation.7 | async-start | bytes 1048576 | tf_op jit(solution)/shard_map/all_to_all | solution.py:82
  464.2 42.2 %all-reduce.11.cloned.1.call-start = ((), (), s32[]{:S(2)}) async-start(), calls=%async_computation.10 | async-start | bytes 524288 | tf_op jit(solution)/shard_map/psum | solution.py:91
Sparse Core Ops, SparseCore 0:
  202.1 31.3 all-reduce.6
  339.6 30.4 all-reduce.8
  475.9 30.4 all-reduce.10
where the time goes:
time: 561 us; the launch traced here: 560 us
  waiting for transfers between devices  231 us (41%)
  blocking collectives  133 us (24%)
  matrix products  80.9 us (14%)
  local copies, waits for them, and re-layouts  43.4 us (8%)
  starting transfers between devices  34.9 us (6%)
  other arithmetic  21.7 us (4%)
  between operations  14.1 us (3%)
    psum x4, blocking collectives, gram_sums(): return lax.psum(values, 'wide')  133 us
    psum x3, waiting for transfers between devices, per_device(): summed_blocks = lax.psum(summed_blocks, 'narrow')  91.8 us
    all_to_all x1, waiting for transfers between devices, per_device(): lax.all_to_all(unit[local_ids], 'wide', split_axis=0, concat_axis=0, tile...  87.2 us
    all_to_all x3, waiting for transfers between devices, per_device(): lax.all_to_all(to_second.reshape(wide_count, capacity, vec_rows * BS), 'w...  29.2 us
    dot_general x6, matrix products, tile_terms(): jnp.einsum('pab,prb->pra', kernel_values, second_vec, precision=HIGH)  28.5 us
    all_to_all x3, waiting for transfers between devices, per_device(): lax.all_to_all(rows[local_ids], 'wide', split_axis=0, concat_axis=0, tile...  23.1 us
    dot_general x6, matrix products, tile_terms(): jnp.einsum('paf,pbf->pab', first_pts, second_pts, preferred_element_type=...  17.6 us
    dot_general x6, matrix products, tile_terms(): jnp.einsum('pab,pra->prb', kernel_values, first_vec, precision=HIGH)  16.5 us
  transfers between devices with their start and end apart: 11, of which 10 were waited for; matrix products, arithmetic and copies ran while one was open for 4% of the time, Pallas kernels for 0%

commit v1 on v0

--- a/solution.py
+++ b/solution.py
@@ -88,7 +88,11 @@
         )
         terms = jnp.concatenate([to_first, returned.reshape(pair_count, vec_rows * BS)], axis=0)
         summed_blocks = jnp.dot(owners, terms, precision=HIGH)
-        summed_blocks = lax.psum(summed_blocks, "narrow")
+        summed_blocks = summed_blocks
+        for hop in (1, 2):
+            summed_blocks = summed_blocks + lax.ppermute(
+                summed_blocks, "narrow", [(dev, dev ^ hop) for dev in range(4)]
+            )
         image = summed_blocks.reshape(-1, vec_rows, BS).transpose(1, 0, 2).reshape(vec_rows, -1)
         residual = image - jnp.dot(last.T, previous, precision=HIGH)
         raw, cross, basis_gram = gram_sums(

time: 561 us -> 475 us (0.85)
  waiting for transfers between devices: 231 us -> 164 us
  between operations: 14.1 us -> 1.05 us
    psum x3 -> x0, waiting for transfers between devices: 91.8 us -> none  [per_device(): summed_blocks = lax.psum(summed_blocks, 'narrow')]
    ppermute x0 -> x6, waiting for transfers between devices: none -> 23.6 us  [per_device(): lax.ppermute(summed_blocks, 'narrow', [(dev, dev ^ hop) for dev in range(...]
  transfers between devices with their start and end apart: 11 -> 14, of which waited for: 10 -> 13; matrix products, arithmetic and copies ran while one was open for 4% -> 5% of each run, Pallas kernels for 0% -> 0%
where the time goes in v1:
time: 475 us; the launch traced here: 474 us
  waiting for transfers between devices  164 us (35%)
  blocking collectives  128 us (27%)
  matrix products  78.2 us (16%)
  local copies, waits for them, and re-layouts  41.2 us (9%)
  starting transfers between devices  39.8 us (8%)
  other arithmetic  22.1 us (5%)
    psum x4, blocking collectives, gram_sums(): return lax.psum(values, 'wide')  128 us
    all_to_all x1, waiting for transfers between devices, per_device(): lax.all_to_all(unit[local_ids], 'wide', split_axis=0, concat_axis=0, tile...  87.2 us
    all_to_all x3, waiting for transfers between devices, per_device(): lax.all_to_all(to_second.reshape(wide_count, capacity, vec_rows * BS), 'w...  29.8 us
    dot_general x6, matrix products, tile_terms(): jnp.einsum('pab,prb->pra', kernel_values, second_vec, precision=HIGH)  28.5 us
    ppermute x6, waiting for transfers between devices, per_device(): lax.ppermute(summed_blocks, 'narrow', [(dev, dev ^ hop) for dev in range(...  23.6 us
    all_to_all x3, waiting for transfers between devices, per_device(): lax.all_to_all(rows[local_ids], 'wide', split_axis=0, concat_axis=0, tile...  23 us
    dot_general x6, matrix products, tile_terms(): jnp.einsum('paf,pbf->pab', first_pts, second_pts, preferred_element_type=...  17.6 us
    dot_general x6, matrix products, tile_terms(): jnp.einsum('pab,pra->prb', kernel_values, first_vec, precision=HIGH)  16.5 us
  transfers between devices with their start and end apart: 14, of which 13 were waited for; matrix products, arithmetic and copies ran while one was open for 5% of the time, Pallas kernels for 0%

profile of v1, /device:TPU:0, one launch (start us, length us, event | category | flops | bytes accessed | tf_op | source)
XLA Modules:
  0.0 473.9 jit_solution(223559767498268323)
XLA Ops:
  2.1 7.3 %all-to-all-start = ((s32[8,1,8]{2,1,0:T(1,128)}), s32[8,1,8]{2,1,0:T(1,128)S(1)}, u32[]{:S(2)}, u32[]{:S(2)}) async-start(s32[8,1,8]{2,1,0:T(1,128)} %bitcast.22), calls=%async_computation | async-start | bytes 8192 | tf_op jit(solution)/shard_map/all_to_all | solution.py:43
  9.8 22.1 %psum.70 = f32[16,16]{1,0:T(8,128)S(1)} all-reduce(f32[16,16]{1,0:T(8,128)S(1)} %fusion.190), channel_id=1, replica_groups=mesh['wide'=8,'narrow'=4] {'wide'}, use_global_device_ids=true, to_apply=%region_1.0 | all-reduce | flops 256 | bytes 2048 | tf_op jit(solution)/shard_map/psum | solution.py:62
  48.6 5.6 %all-to-all-done.1 = f32[8,8,16,128]{3,2,1,0:T(8,128)S(1)} async-done(((f32[8,8,16,128]{3,2,1,0:T(8,128)}), f32[8,8,16,128]{3,2,1,0:T(8,128)S(1)}, u32[]{:S(2)}, u32[]{:S(2)}) %all-to-all-start.1) | async-done | bytes 524320 | tf_op jit(solution)/shard_map/all_to_all | solution.py:73
  54.2 4.7 all-to-all-start.2
  60.5 87.2 %all-to-all-done.2 = bf16[8,8,128,256]{3,2,1,0:T(8,128)(2,1)} async-done(((bf16[8,8,128,256]{3,2,1,0:T(8,128)(2,1)}), bf16[8,8,128,256]{3,2,1,0:T(8,128)(2,1)}, u32[]{:S(2)}, u32[]{:S(2)}) %all-to-all-start.2) | async-done | bytes 4194336 | tf_op jit(solution)/shard_map/all_to_all | solution.py:46
  149.4 23.6 %while.42 = (s32[]{:T(128)}, f32[2,32,16,128]{3,2,1,0:T(8,128)}, f32[2,32,16,128]{3,2,1,0:T(8,128)}, f32[2,32,16,128]{3,2,1,0:T(8,128)S(1)}, s32[2,32]{1,0:T(2,1...) while((s32[]{:T(128)}, f32[2,32,16,128]{3,2,1,0:T(8,128)}, ...), condition=%wide.region_5.8_spmd, body=%wide.region_4.7_spmd.sunk | while | flops 471860320 | bytes 17833084 | solution.py:77
  180.6 12.5 %all-to-all-done.3 = f32[8,8,2048]{2,1,0:T(8,128)S(1)} async-done(((f32[8,8,2048]{2,1,0:T(8,128)}), f32[8,8,2048]{2,1,0:T(8,128)S(1)}, u32[]{:S(2)}, u32[]{:S(2)}) %all-to-all-start.3) | async-done | bytes 524320 | tf_op jit(solution)/shard_map/all_to_all | solution.py:82
  198.3 6.3 %collective-permute-done.1 = f32[32,2048]{1,0:T(8,128)S(1)} collective-permute-done((f32[32,2048]{1,0:T(8,128)S(1)}, f32[32,2048]{1,0:T(8,128)S(1)}, u32[]{:S(2)}, u32[]{:S(2)}) %collective-permute-start.1) | collective-permute-done | bytes 262176 | tf_op jit(solution)/shard_map/ppermute | solution.py:93
  205.9 35.2 %all-reduce.2 = (f32[16,16]{1,0:T(8,128)S(1)}, f32[16,16]{1,0:T(8,128)S(1)}, f32[16,16]{1,0:T(8,128)S(1)}) all-reduce(f32[16,16]{1,0:T(8,128)S(1)} %fusion.192, f32[16,16]{1,0:T(8,128)S(1)} %fusion.191, f32[16,16]{1,0:T(8,128)S(1)} %fusion.193), channel_id=1, replica_groups=mesh['wide'=8,'narrow'=4] {'wide'}, use_global_device_ids=true, to_apply=%region_7.10 | all-reduce | flops 768 | bytes 6144 | tf_op jit(solution)/shard_map/psum | solution.py:62
  253.8 8.8 %all-to-all-done.4 = f32[8,8,16,128]{3,2,1,0:T(8,128)} async-done(((f32[8,8,16,128]{3,2,1,0:T(8,128)}), f32[8,8,16,128]{3,2,1,0:T(8,128)}, u32[]{:S(2)}, u32[]{:S(2)}) %all-to-all-start.4) | async-done | bytes 524320 | tf_op jit(solution)/shard_map/all_to_all | solution.py:73
  264.2 25.6 %while.43 = (s32[]{:T(128)}, f32[2,32,16,128]{3,2,1,0:T(8,128)}, f32[2,32,16,128]{3,2,1,0:T(8,128)}, f32[2,32,16,128]{3,2,1,0:T(8,128)}, s32[2,32]{1,0:T(2,128)S...) while((s32[]{:T(128)}, f32[2,32,16,128]{3,2,1,0:T(8,128)}, ...), condition=%wide.region_10.13_spmd, body=%wide.region_9.12_spmd.sunk | while | flops 471860320 | bytes 17833084 | solution.py:77
  269.2 5.1 %fusion.276 = f32[2,32,16,128]{3,2,1,0:T(8,128)} fusion(f32[2,32,16,128]{3,2,1,0:T(8,128)} %get-tuple-element.571, s32[]{:T(128)} %get-tuple-element.570, f32[32,128,128]{2,1,0:T(8,128)S(1)} %fusion.275, f32[2,32,16,128]{3,2,1,0:T(8,128)} %get-tuple-element.582), kind=kOutput, calls=%fused_computation.47.clone.1 | convolution fusion | flops 101711872 | bytes 2622464 | tf_op jit(solution)/shard_map/while/body/eval_jaxpr/pab,prb->pra/dot_general | solution.py:25
  282.0 5.1 %fusion.276 = f32[2,32,16,128]{3,2,1,0:T(8,128)} fusion(f32[2,32,16,128]{3,2,1,0:T(8,128)} %get-tuple-element.571, s32[]{:T(128)} %get-tuple-element.570, f32[32,128,128]{2,1,0:T(8,128)S(1)} %fusion.275, f32[2,32,16,128]{3,2,1,0:T(8,128)} %get-tuple-element.582), kind=kOutput, calls=%fused_computation.47.clone.1 | convolution fusion | flops 101711872 | bytes 2622464 | tf_op jit(solution)/shard_map/while/body/eval_jaxpr/pab,prb->pra/dot_general | solution.py:25
  297.4 8.3 %all-to-all-done.5 = f32[8,8,2048]{2,1,0:T(8,128)S(1)} async-done(((f32[8,8,2048]{2,1,0:T(8,128)}), f32[8,8,2048]{2,1,0:T(8,128)S(1)}, u32[]{:S(2)}, u32[]{:S(2)}) %all-to-all-start.5) | async-done | bytes 524320 | tf_op jit(solution)/shard_map/all_to_all | solution.py:82
  310.9 6.4 %collective-permute-done.3 = f32[32,2048]{1,0:T(8,128)S(1)} collective-permute-done((f32[32,2048]{1,0:T(8,128)S(1)}, f32[32,2048]{1,0:T(8,128)S(1)}, u32[]{:S(2)}, u32[]{:S(2)}) %collective-permute-start.3) | collective-permute-done | bytes 262176 | tf_op jit(solution)/shard_map/ppermute | solution.py:93
  319.3 35.3 %all-reduce.1 = (f32[16,16]{1,0:T(8,128)S(1)}, f32[16,16]{1,0:T(8,128)S(1)}, f32[16,16]{1,0:T(8,128)S(1)}) all-reduce(f32[16,16]{1,0:T(8,128)S(1)} %fusion.195, f32[16,16]{1,0:T(8,128)S(1)} %fusion.194, f32[16,16]{1,0:T(8,128)S(1)} %fusion.196), channel_id=1, replica_groups=mesh['wide'=8,'narrow'=4] {'wide'}, use_global_device_ids=true, to_apply=%region_12.15 | all-reduce | flops 768 | bytes 6144 | tf_op jit(solution)/shard_map/psum | solution.py:62
  361.6 4.4 all-to-all-start.6
  367.4 8.6 %all-to-all-done.6 = f32[8,8,16,128]{3,2,1,0:T(8,128)} async-done(((f32[8,8,16,128]{3,2,1,0:T(8,128)}), f32[8,8,16,128]{3,2,1,0:T(8,128)}, u32[]{:S(2)}, u32[]{:S(2)}) %all-to-all-start.6) | async-done | bytes 524320 | tf_op jit(solution)/shard_map/all_to_all | solution.py:73
  377.7 25.6 %while.44 = (s32[]{:T(128)}, f32[2,32,16,128]{3,2,1,0:T(8,128)}, f32[2,32,16,128]{3,2,1,0:T(8,128)}, f32[2,32,16,128]{3,2,1,0:T(8,128)}, s32[2,32]{1,0:T(2,128)S...) while((s32[]{:T(128)}, f32[2,32,16,128]{3,2,1,0:T(8,128)}, ...), condition=%wide.region_15.18_spmd, body=%wide.region_14.17_spmd.sunk | while | flops 471860320 | bytes 17833084 | solution.py:77
  382.7 5.1 %fusion.284 = f32[2,32,16,128]{3,2,1,0:T(8,128)} fusion(f32[2,32,16,128]{3,2,1,0:T(8,128)} %get-tuple-element.598, s32[]{:T(128)} %get-tuple-element.597, f32[32,128,128]{2,1,0:T(8,128)S(1)} %fusion.283, f32[2,32,16,128]{3,2,1,0:T(8,128)} %get-tuple-element.609), kind=kOutput, calls=%fused_computation.77.clone.1 | convolution fusion | flops 101711872 | bytes 2622464 | tf_op jit(solution)/shard_map/while/body/eval_jaxpr/pab,prb->pra/dot_general | solution.py:25
  395.5 5.1 %fusion.284 = f32[2,32,16,128]{3,2,1,0:T(8,128)} fusion(f32[2,32,16,128]{3,2,1,0:T(8,128)} %get-tuple-element.598, s32[]{:T(128)} %get-tuple-element.597, f32[32,128,128]{2,1,0:T(8,128)S(1)} %fusion.283, f32[2,32,16,128]{3,2,1,0:T(8,128)} %get-tuple-element.609), kind=kOutput, calls=%fused_computation.77.clone.1 | convolution fusion | flops 101711872 | bytes 2622464 | tf_op jit(solution)/shard_map/while/body/eval_jaxpr/pab,prb->pra/dot_general | solution.py:25
  410.1 9.1 %all-to-all-done.7 = f32[8,8,2048]{2,1,0:T(8,128)S(1)} async-done(((f32[8,8,2048]{2,1,0:T(8,128)}), f32[8,8,2048]{2,1,0:T(8,128)S(1)}, u32[]{:S(2)}, u32[]{:S(2)}) %all-to-all-start.7) | async-done | bytes 524320 | tf_op jit(solution)/shard_map/all_to_all | solution.py:82
  423.3 6.3 %collective-permute-done.5 = f32[32,2048]{1,0:T(8,128)S(1)} collective-permute-done((f32[32,2048]{1,0:T(8,128)S(1)}, f32[32,2048]{1,0:T(8,128)S(1)}, u32[]{:S(2)}, u32[]{:S(2)}) %collective-permute-start.5) | collective-permute-done | bytes 262176 | tf_op jit(solution)/shard_map/ppermute | solution.py:93
  431.8 35.3 %all-reduce = (f32[16,16]{1,0:T(8,128)S(1)}, f32[16,16]{1,0:T(8,128)S(1)}, f32[16,16]{1,0:T(8,128)S(1)}) all-reduce(f32[16,16]{1,0:T(8,128)S(1)} %fusion.198, f32[16,16]{1,0:T(8,128)S(1)} %fusion.197, f32[16,16]{1,0:T(8,128)S(1)} %fusion.199), channel_id=1, replica_groups=mesh['wide'=8,'narrow'=4] {'wide'}, use_global_device_ids=true, to_apply=%region_17.20 | all-reduce | flops 768 | bytes 6144 | tf_op jit(solution)/shard_map/psum | solution.py:62
  (177 shorter events, 149.3 us)
Async XLA Ops:
  0.6 8.8 %copy-start = (f32[16,4096]{1,0:T(8,128)S(1)}, f32[16,4096]{1,0:T(8,128)}, u32[]{:S(2)}) copy-start(f32[16,4096]{1,0:T(8,128)} %param.13) | copy-start | bytes 786436
  2.1 36.7 %all-to-all-start = ((s32[8,1,8]{2,1,0:T(1,128)}), s32[8,1,8]{2,1,0:T(1,128)S(1)}, u32[]{:S(2)}, u32[]{:S(2)}) async-start(s32[8,1,8]{2,1,0:T(1,128)} %bitcast.22), calls=%async_computation | async-start | bytes 8192 | tf_op jit(solution)/shard_map/all_to_all | solution.py:43
  40.4 13.8 %all-to-all-start.1 = ((f32[8,8,16,128]{3,2,1,0:T(8,128)}), f32[8,8,16,128]{3,2,1,0:T(8,128)S(1)}, u32[]{:S(2)}, u32[]{:S(2)}) async-start(f32[8,8,16,128]{3,2,1,0:T(8,128)} %bitcast.29), calls=%async_computation.1 | async-start | bytes 1048576 | tf_op jit(solution)/shard_map/all_to_all | solution.py:73
  54.2 4.7 copy-start.4
  54.2 93.5 %all-to-all-start.2 = ((bf16[8,8,128,256]{3,2,1,0:T(8,128)(2,1)}), bf16[8,8,128,256]{3,2,1,0:T(8,128)(2,1)}, u32[]{:S(2)}, u32[]{:S(2)}) async-start(bf16[8,8,128,256]{3,2,1,0:T(8,128)(2,1)} %bitcast.309), calls=%async_computation.2 | async-start | bytes 8388608 | tf_op jit(solution)/shard_map/all_to_all | solution.py:46
  154.3 4.1 copy-start.2
  166.1 4.1 copy-start.2
  174.9 18.2 %all-to-all-start.3 = ((f32[8,8,2048]{2,1,0:T(8,128)}), f32[8,8,2048]{2,1,0:T(8,128)S(1)}, u32[]{:S(2)}, u32[]{:S(2)}) async-start(f32[8,8,2048]{2,1,0:T(8,128)} %reshape.254), calls=%async_computation.3 | async-start | bytes 1048576 | tf_op jit(solution)/shard_map/all_to_all | solution.py:82
  194.6 1.6 collective-permute-start
  196.2 8.4 %collective-permute-start.1 = (f32[32,2048]{1,0:T(8,128)S(1)}, f32[32,2048]{1,0:T(8,128)S(1)}, u32[]{:S(2)}, u32[]{:S(2)}) collective-permute-start(f32[32,2048]{1,0:T(8,128)S(1)} %add.164), channel_id=1, source_target_pairs={{0,2},{1,3},{2,0},{3,1},{4,6},{5,7},{6,4},{7,5},{8,10},{9,11},{10,... | collective-permute-start | bytes 786440 | tf_op jit(solution)/shard_map/ppermute | solution.py:93
  248.2 14.4 %all-to-all-start.4 = ((f32[8,8,16,128]{3,2,1,0:T(8,128)}), f32[8,8,16,128]{3,2,1,0:T(8,128)}, u32[]{:S(2)}, u32[]{:S(2)}) async-start(f32[8,8,16,128]{3,2,1,0:T(8,128)} %bitcast.321), calls=%async_computation.4 | async-start | bytes 1048576 | tf_op jit(solution)/shard_map/all_to_all | solution.py:73
  269.2 5.1 %copy-start.3 = (f32[2,32,16,128]{3,2,1,0:T(8,128)S(1)}, f32[2,32,16,128]{3,2,1,0:T(8,128)}, u32[]{:S(2)}) copy-start(f32[2,32,16,128]{3,2,1,0:T(8,128)} %get-tuple-element.586) | copy-start | bytes 1572868 | tf_op jit(solution)/shard_map/while
  282.0 5.1 %copy-start.3 = (f32[2,32,16,128]{3,2,1,0:T(8,128)S(1)}, f32[2,32,16,128]{3,2,1,0:T(8,128)}, u32[]{:S(2)}) copy-start(f32[2,32,16,128]{3,2,1,0:T(8,128)} %get-tuple-element.586) | copy-start | bytes 1572868 | tf_op jit(solution)/shard_map/while
  291.7 14.0 %all-to-all-start.5 = ((f32[8,8,2048]{2,1,0:T(8,128)}), f32[8,8,2048]{2,1,0:T(8,128)S(1)}, u32[]{:S(2)}, u32[]{:S(2)}) async-start(f32[8,8,2048]{2,1,0:T(8,128)} %reshape.261), calls=%async_computation.5 | async-start | bytes 1048576 | tf_op jit(solution)/shard_map/all_to_all | solution.py:82
  307.2 1.6 collective-permute-start.2
  308.8 8.4 %collective-permute-start.3 = (f32[32,2048]{1,0:T(8,128)S(1)}, f32[32,2048]{1,0:T(8,128)S(1)}, u32[]{:S(2)}, u32[]{:S(2)}) collective-permute-start(f32[32,2048]{1,0:T(8,128)S(1)} %add.167), channel_id=1, source_target_pairs={{0,2},{1,3},{2,0},{3,1},{4,6},{5,7},{6,4},{7,5},{8,10},{9,11},{10,... | collective-permute-start | bytes 786440 | tf_op jit(solution)/shard_map/ppermute | solution.py:93
  361.6 14.4 %all-to-all-start.6 = ((f32[8,8,16,128]{3,2,1,0:T(8,128)}), f32[8,8,16,128]{3,2,1,0:T(8,128)}, u32[]{:S(2)}, u32[]{:S(2)}) async-start(f32[8,8,16,128]{3,2,1,0:T(8,128)} %bitcast.320), calls=%async_computation.6 | async-start | bytes 1048576 | tf_op jit(solution)/shard_map/all_to_all | solution.py:73
  382.7 5.1 %copy-start.1 = (f32[2,32,16,128]{3,2,1,0:T(8,128)S(1)}, f32[2,32,16,128]{3,2,1,0:T(8,128)}, u32[]{:S(2)}) copy-start(f32[2,32,16,128]{3,2,1,0:T(8,128)} %get-tuple-element.613) | copy-start | bytes 1572868 | tf_op jit(solution)/shard_map/while
  395.5 5.1 %copy-start.1 = (f32[2,32,16,128]{3,2,1,0:T(8,128)S(1)}, f32[2,32,16,128]{3,2,1,0:T(8,128)}, u32[]{:S(2)}) copy-start(f32[2,32,16,128]{3,2,1,0:T(8,128)} %get-tuple-element.613) | copy-start | bytes 1572868 | tf_op jit(solution)/shard_map/while
  405.2 13.9 %all-to-all-start.7 = ((f32[8,8,2048]{2,1,0:T(8,128)}), f32[8,8,2048]{2,1,0:T(8,128)S(1)}, u32[]{:S(2)}, u32[]{:S(2)}) async-start(f32[8,8,2048]{2,1,0:T(8,128)} %reshape.268), calls=%async_computation.7 | async-start | bytes 1048576 | tf_op jit(solution)/shard_map/all_to_all | solution.py:82
  419.6 1.6 collective-permute-start.4
  421.3 8.4 %collective-permute-start.5 = (f32[32,2048]{1,0:T(8,128)S(1)}, f32[32,2048]{1,0:T(8,128)S(1)}, u32[]{:S(2)}, u32[]{:S(2)}) collective-permute-start(f32[32,2048]{1,0:T(8,128)S(1)} %add.170), channel_id=1, source_target_pairs={{0,2},{1,3},{2,0},{3,1},{4,6},{5,7},{6,4},{7,5},{8,10},{9,11},{10,... | collective-permute-start | bytes 786440 | tf_op jit(solution)/shard_map/ppermute | solution.py:93
